TPU v7x, 128 devices: a whole 4x4x4 slice. The times are simulated.
128 devices in a mesh: gx: 8 (over z, core), gy: 16 (over x, y).
Axes of the slice: x: 4, y: 4, z: 4, core: 2. Of those that a mesh axis runs over, the one named last changes fastest.
Arguments:
- tokens: bfloat16 [4096, 4096], P(('gx', 'gy')), may hold values from -3 to 3
- attn_gain: bfloat16 [4096], replicated, may hold values from 0.099609375 to 1.8984375
- mlp_gain: bfloat16 [4096], replicated, may hold values from 0.099609375 to 1.8984375
- w_query: bfloat16 [4096, 4096], P('gx', 'gy'), may hold values from -1 to 1
- w_key: bfloat16 [4096, 1024], P('gx', 'gy'), may hold values from -1 to 1
- value_projection: bfloat16 [4096, 1024], P('gx', 'gy'), may hold values from -0.09375 to 0.09375
- w_out: bfloat16 [4096, 4096], P('gy', 'gx'), may hold values from -0.09375 to 0.09375
- w_gate: bfloat16 [4096, 14336], P('gx', 'gy'), may hold values from -0.09375 to 0.09375
- w_up: bfloat16 [4096, 14336], P('gx', 'gy'), may hold values from -0.09375 to 0.09375
- w_down: bfloat16 [14336, 4096], P('gy', 'gx'), may hold values from -0.046875 to 0.046875
- lengths: int32 [6], replicated, may hold values from 1 to 3072, 4096 in all
- page_table: int32 [128, 2], replicated, may hold values from 0 to 15, as said below
Outputs:
- layer_out: bfloat16 [4096, 4096], P(('gx', 'gy'))
- paged_key_value_cache: bfloat16 [128, 2, 32, 1024], P('gx', None, None, 'gy')
Inputs may be any that keep to these rules, and one draw needn't show every extreme that they name: `page_table`: page p belongs to token group p // 16, the tokens of one index of gx. Its owner is an index of gx and its slot is below 16; every pair of owner and slot is taken by exactly one page. Of one token group's pages, 8 owners receive exactly 2 each and the other owners none.
All inputs are finite; a program needn't handle non-finite values.
Results may differ from a plain program's by a relative error of at most 0.025.
The roundings to bfloat16 on the way count: a program that leaves them out, or rounds other values in their place, can miss the bound.
Values may be sent and summed in bfloat16 or wider, within the bound.
A program may use at most 128 MiB of HBM per device.

v0:
```python
import jax
import jax.numpy as jnp
from jax import lax
from jax.sharding import PartitionSpec as P

HEAD_WIDTH = 128
WIN = 4096
PAGE_TOKENS = 32
rope_base = 10000.0
norm_eps = 1e-05
masked_score = -1e30


def partner(value, axis, distance):
    mask = 2**distance
    pairs = [(source, source ^ mask) for source in range(lax.axis_size(axis))]
    return lax.ppermute(value, axis, pairs)


def rms_scale(values, gain):
    floats = values.astype(jnp.float32)
    mean_square = jnp.mean(floats * floats, axis=-1, keepdims=True)
    return floats * lax.rsqrt(mean_square + norm_eps) * gain.astype(jnp.float32)


def segment_info(lengths, token_index):
    ends = jnp.cumsum(lengths, dtype=jnp.int32)
    starts = ends - lengths
    inside = (token_index[:, None] >= starts[None, :]).astype(jnp.int32)
    segment = jnp.sum(inside, axis=1, dtype=jnp.int32) - 1
    chosen = (segment[:, None] == jnp.arange(lengths.shape[0], dtype=jnp.int32)[None, :]).astype(
        jnp.int32
    )
    token_positions = token_index - jnp.sum(chosen * starts[None, :], axis=1, dtype=jnp.int32)
    return (segment, token_positions)


def apply_rotary(values, token_positions):
    half = values.shape[-1] // 2
    freq = rope_base ** (-jnp.arange(half, dtype=jnp.float32) * 2.0 / values.shape[-1])
    angle = token_positions.astype(jnp.float32)[:, None] * freq[None, :]
    cosine = jnp.cos(angle)[:, None, :]
    sine = jnp.sin(angle)[:, None, :]
    first = values[..., :half]
    second = values[..., half:]
    return jnp.concatenate(
        [first * cosine - second * sine, second * cosine + first * sine], axis=-1
    )


def join_halves(mine, other, lower):
    return jnp.where(
        lower, jnp.concatenate([mine, other], axis=1), jnp.concatenate([other, mine], axis=1)
    )


def row_products(source, pieces):
    return tuple((jnp.dot(source, piece, preferred_element_type=jnp.float32) for piece in pieces))


def per_device(
    tokens,
    attn_gain,
    mlp_gain,
    w_query,
    w_key,
    value_projection,
    w_out,
    w_gate,
    w_up,
    w_down,
    lengths,
    page_table,
):
    group_count = lax.axis_size("gx")
    local_rows = tokens.shape[0]
    group = local_rows * lax.axis_size("gy")
    group_index = lax.axis_index("gx")
    head_index = lax.axis_index("gy")
    group_start = group_index * group
    lower = head_index % 2 == 0
    query_cols = w_query.shape[1]
    query_heads = query_cols // HEAD_WIDTH
    key_cols = w_key.shape[1]
    key_heads = max(1, key_cols // HEAD_WIDTH)
    per_key = query_heads // key_heads
    normed = lax.all_gather(
        rms_scale(tokens, attn_gain).astype(jnp.bfloat16), "gy", axis=0, tiled=True
    )
    query = row_products(normed, (lax.all_gather(w_query, "gx", axis=0, tiled=True),))[0]
    key_weight, value_weight = (w_key, value_projection)
    unrotated_key, value_raw = row_products(
        normed,
        (
            lax.all_gather(key_weight, "gx", axis=0, tiled=True),
            lax.all_gather(value_weight, "gx", axis=0, tiled=True),
        ),
    )
    other_key, other_value = (
        partner(unrotated_key.astype(jnp.bfloat16), "gy", 0).astype(unrotated_key.dtype),
        partner(value_raw.astype(jnp.bfloat16), "gy", 0).astype(value_raw.dtype),
    )
    unrotated_key = join_halves(unrotated_key, other_key, lower)
    value_raw = join_halves(value_raw, other_value, lower)
    token_index = group_start + jnp.arange(group, dtype=jnp.int32)
    segment, token_positions = segment_info(lengths, token_index)
    query_rot = (
        apply_rotary(query.reshape(group, query_heads, HEAD_WIDTH), token_positions)
        .astype(jnp.bfloat16)
        .reshape(group, key_heads, per_key, HEAD_WIDTH)
    )
    rotated_key = (
        apply_rotary(unrotated_key.reshape(group, key_heads, HEAD_WIDTH), token_positions)
        .astype(jnp.bfloat16)
        .reshape(group, key_heads * HEAD_WIDTH)
    )
    value_vectors = value_raw.astype(jnp.bfloat16)
    scale = HEAD_WIDTH ** (-0.5)
    start_state = (
        jnp.full((key_heads, per_key, group), masked_score, jnp.float32),
        jnp.zeros((key_heads, per_key, group), jnp.float32),
        jnp.zeros((key_heads, per_key, group, HEAD_WIDTH), jnp.float32),
    )
    keys = lax.all_gather(rotated_key, "gx", axis=0, tiled=True)
    values = lax.all_gather(value_vectors, "gx", axis=0, tiled=True)
    count = keys.shape[0]
    key_index = jnp.arange(count, dtype=jnp.int32)
    key_segment, unused = segment_info(lengths, key_index)
    distance = token_index[:, None] - key_index[None, :]
    allowed = (segment[:, None] == key_segment[None, :]) & (distance >= 0) & (distance < WIN)

    def update(state):
        running, total, weighted = state
        scores = (
            jnp.einsum(
                "qhgd,khd->hgqk",
                query_rot,
                keys.reshape(count, key_heads, HEAD_WIDTH),
                preferred_element_type=jnp.float32,
            )
            * scale
        )
        masked = jnp.where(allowed[None, None], scores, masked_score)
        newest = jnp.maximum(running, jnp.max(masked, axis=-1))
        weights = jnp.where(allowed[None, None], jnp.exp(masked - newest[..., None]), 0.0)
        mixed = jnp.einsum(
            "hgqk,khd->hgqd",
            weights.astype(jnp.bfloat16),
            values.reshape(count, key_heads, HEAD_WIDTH),
            preferred_element_type=jnp.float32,
        )
        return (newest, jnp.sum(weights, axis=-1), mixed)

    state = lax.cond(jnp.any(allowed), update, lambda state: state, start_state)
    attended = (state[2] / state[1][..., None]).astype(jnp.bfloat16)
    attended = attended.transpose(2, 0, 1, 3).reshape(group, query_cols)
    partial_value = jnp.dot(
        attended,
        lax.all_gather(w_out, "gx", axis=1, tiled=True),
        preferred_element_type=jnp.float32,
    )
    share = lax.psum_scatter(
        partial_value.astype(jnp.bfloat16), "gy", scatter_dimension=0, tiled=True
    ).astype(jnp.float32)
    residual = (tokens.astype(jnp.float32) + share).astype(jnp.bfloat16)
    mlp_input = lax.all_gather(
        rms_scale(residual, mlp_gain).astype(jnp.bfloat16), "gy", axis=0, tiled=True
    )
    gate, up_values = row_products(
        mlp_input,
        (
            lax.all_gather(w_gate, "gx", axis=0, tiled=True),
            lax.all_gather(w_up, "gx", axis=0, tiled=True),
        ),
    )
    hidden = (jax.nn.silu(gate) * up_values).astype(jnp.bfloat16)
    down_full = lax.all_gather(w_down, "gx", axis=1, tiled=True)
    mlp_share = lax.psum_scatter(
        jnp.dot(hidden, down_full, preferred_element_type=jnp.float32).astype(jnp.bfloat16),
        "gy",
        scatter_dimension=0,
        tiled=True,
    ).astype(jnp.float32)
    layer_out = (residual.astype(jnp.float32) + mlp_share).astype(jnp.bfloat16)
    own_start = jnp.where(lower, 0, key_cols).astype(jnp.int32)
    local_key = lax.dynamic_slice_in_dim(rotated_key, own_start, key_cols, 1)
    own_value = lax.dynamic_slice_in_dim(value_vectors, own_start, key_cols, 1)
    slots_group = group // PAGE_TOKENS
    capacity = max(2, slots_group // group_count)
    pages_local = (
        jnp.stack([local_key, own_value], axis=0)
        .reshape(2, slots_group, PAGE_TOKENS, key_cols)
        .transpose(1, 0, 2, 3)
        .reshape(slots_group, 2 * PAGE_TOKENS * key_cols)
    )
    owner = page_table[:, 0]
    slot = page_table[:, 1]
    page_index = jnp.arange(owner.shape[0], dtype=jnp.int32)
    page_group = page_index // slots_group
    before = (
        (page_group[:, None] == page_group[None, :])
        & (owner[:, None] == owner[None, :])
        & (page_index[None, :] < page_index[:, None])
    )
    rank = jnp.sum(before.astype(jnp.int32), axis=1, dtype=jnp.int32)
    my_owner = lax.dynamic_slice_in_dim(owner, group_index * slots_group, slots_group, 0)
    my_rank = lax.dynamic_slice_in_dim(rank, group_index * slots_group, slots_group, 0)
    target = jnp.arange(group_count * capacity, dtype=jnp.int32)
    select = (
        (my_owner[None, :] == target[:, None] // capacity)
        & (my_rank[None, :] == target[:, None] % capacity)
    ).astype(jnp.bfloat16)
    outgoing = (
        jnp.dot(select, pages_local, preferred_element_type=jnp.float32)
        .astype(jnp.bfloat16)
        .reshape(group_count, capacity, 2, PAGE_TOKENS, key_cols)
    )
    incoming = lax.all_to_all(outgoing, "gx", split_axis=0, concat_axis=0, tiled=True)
    column = page_group * capacity + rank
    pick = (
        (owner[None, :] == group_index)
        & (slot[None, :] == jnp.arange(slots_group, dtype=jnp.int32)[:, None])
    ).astype(jnp.float32)
    place = (column[:, None] == target[None, :]).astype(jnp.float32)
    routing = jnp.dot(pick, place, preferred_element_type=jnp.float32).astype(jnp.bfloat16)
    paged_key_value_cache = (
        jnp.dot(
            routing,
            incoming.reshape(group_count * capacity, 2 * PAGE_TOKENS * key_cols),
            preferred_element_type=jnp.float32,
        )
        .astype(jnp.bfloat16)
        .reshape(slots_group, 2, PAGE_TOKENS, key_cols)
    )
    return (layer_out, paged_key_value_cache)


def solution(mesh):
    placed = (
        P(("gx", "gy"), None),
        P(),
        P(),
        P("gx", "gy"),
        P("gx", "gy"),
        P("gx", "gy"),
        P("gy", "gx"),
        P("gx", "gy"),
        P("gx", "gy"),
        P("gy", "gx"),
        P(),
        P(),
    )
    return jax.shard_map(
        per_device,
        mesh=mesh,
        in_specs=placed,
        out_specs=(P(("gx", "gy"), None), P("gx", None, None, "gy")),
        check_vma=False,
    )
```

profile of v0, /device:TPU:0, one launch (start us, length us, event | category | flops | bytes accessed | tf_op | source)
XLA Modules:
  0.0 550.2 jit_solution(15981981439846609788)
XLA Ops:
  7.2 0.7 convert_element_type.115
  7.9 1.1 fusion.21
  9.1 1.8 fusion.23
  10.9 0.7 all-gather.12.cloned.1.call-update
  11.7 0.8 reduce-window.9
  12.5 0.7 bitcast_subtract_fusion
  13.4 14.6 %all_gather.35 = bf16[4096,64]{0,1:T(8,128)(2,1)S(1)} all-gather(bf16[512,64]{0,1:T(8,128)(2,1)} %param.18), channel_id=1, replica_groups=mesh['gx'=8,'gy'=16] {'gx'}, dimensions={0}, use_global_device_ids=true | all-gather | bytes 589824 | tf_op jit(solution)/shard_map/all_gather | solution.py:95
  28.0 36.9 %all-gather.10.cloned.1.call-done = bf16[512,4096]{1,0:T(8,128)(2,1)} async-done(((bf16[32,4096]{1,0:T(8,128)(2,1)}), bf16[512,4096]{1,0:T(8,128)(2,1)}) %all-gather.10.cloned.1.call-update) | async-done | bytes 4194320 | tf_op jit(solution)/shard_map/all_gather | solution.py:87
  64.9 3.6 fusion.62
  68.5 1.5 collective-permute-start
  70.0 2.8 collective-permute-done
  72.9 0.6 fusion.37
  73.4 0.7 pad_maximum_fusion.1
  74.2 14.2 %all_gather.37 = bf16[4096,64]{0,1:T(8,128)(2,1)S(1)} all-gather(bf16[512,64]{0,1:T(8,128)(2,1)S(1)} %copy-done.3), channel_id=1, replica_groups=mesh['gx'=8,'gy'=16] {'gx'}, dimensions={0}, use_global_device_ids=true | all-gather | bytes 589824 | tf_op jit(solution)/shard_map/all_gather | solution.py:96
  88.3 3.7 fusion.64
  92.0 1.8 collective-permute-start.1
  93.8 2.6 collective-permute-done.1
  96.4 0.7 fusion.31
  97.2 0.5 all-gather.18.cloned.1.call-update
  97.8 0.1 convert_reduce_fusion
  97.9 3.6 fusion.20
  102.1 1.8 multiply_cosine_fusion
  103.9 4.2 fusion.63
  108.1 0.2 copy.44
  108.3 0.2 copy.45
  108.5 1.2 fusion.29
  109.7 0.1 pad_maximum_fusion
  109.9 7.8 %all-gather.14.cloned.1.call-done = bf16[4096,128]{0,1:T(8,128)(2,1)} async-done(((bf16[512,128]{0,1:T(8,128)(2,1)}), bf16[4096,128]{0,1:T(8,128)(2,1)}) %all-gather.14.cloned.1.call-update) | async-done | bytes 1048592 | tf_op jit(solution)/shard_map/all_gather | solution.py:124
  117.7 25.0 %all-gather.16.cloned.1.call-done = bf16[4096,128]{0,1:T(8,128)(2,1)} async-done(((bf16[512,128]{0,1:T(8,128)(2,1)}), bf16[4096,128]{0,1:T(8,128)(2,1)}) %all-gather.16.cloned.1.call-update) | async-done | bytes 1048592 | tf_op jit(solution)/shard_map/all_gather | solution.py:125
  142.8 14.2 %conditional.1 = (f32[1,2,512]{2,1,0:T(2,128)S(1)}, f32[1,2,512,128]{2,3,1,0:T(8,128)S(1)}) conditional(s32[]{:T(128)} %convert_element_type.114, () %tuple.16, (pred[512,4096]{0,1:T(8,128)(4,1)S(1)}, bf16[512,1,2,128]{3,0,2,1:T(8,128)(2,1)S(1)}, bf16[4096,128]{0,1:T(8,128)(2,1)}, bf16[4096,128]{0,1:T(8,128)(2,1)}) %tuple.17), branch_computations={%region_6.7_spmd, %region_7.10_spmd} | conditional | flops 2202008576 | bytes 63725612 | solution.py:154
  142.8 5.1 fusion
  147.9 4.6 fusion.7
  152.5 4.4 fusion.2
  157.0 12.6 %all-gather.18.cloned.1.call-done = bf16[256,4096]{1,0:T(8,128)(2,1)} async-done(((bf16[256,512]{1,0:T(8,128)(2,1)}), bf16[256,4096]{1,0:T(8,128)(2,1)}) %all-gather.18.cloned.1.call-update) | async-done | bytes 2097168 | tf_op jit(solution)/shard_map/all_gather | solution.py:159
  169.6 4.9 convolution_convert_fusion.1
  174.6 0.7 all-gather.22.cloned.1.call-update
  175.4 77.2 %reduce-scatter.3.cloned.1.call-done = bf16[32,4096]{1,0:T(8,128)(2,1)} async-done(((bf16[512,4096]{1,0:T(8,128)(2,1)}), bf16[32,4096]{1,0:T(8,128)(2,1)}) %reduce-scatter.3.cloned.1.call-update) | async-done | bytes 262160 | tf_op jit(solution)/shard_map/reduce_scatter | solution.py:162
  252.6 1.1 fusion.25
  253.7 1.8 fusion.27
  255.6 0.7 all-gather.24.cloned.1.call-update
  256.3 0.5 all-gather.26.cloned.1.call-update
  256.9 0.3 reduce-scatter.5.cloned.1.call-start
  257.1 42.2 %all-gather.22.cloned.1.call-done = bf16[4096,896]{1,0:T(8,128)(2,1)} async-done(((bf16[512,896]{1,0:T(8,128)(2,1)}), bf16[4096,896]{1,0:T(8,128)(2,1)}) %all-gather.22.cloned.1.call-update) | async-done | bytes 7340048 | tf_op jit(solution)/shard_map/all_gather | solution.py:172
  299.4 54.3 %all-gather.20.cloned.1.call-done = bf16[512,4096]{1,0:T(8,128)(2,1)} async-done(((bf16[32,4096]{1,0:T(8,128)(2,1)}), bf16[512,4096]{1,0:T(8,128)(2,1)}) %all-gather.20.cloned.1.call-update) | async-done | bytes 4194320 | tf_op jit(solution)/shard_map/all_gather | solution.py:166
  353.7 9.8 %fusion.65 = f32[512,896]{1,0:T(8,128)S(1)} fusion(bf16[512,4096]{1,0:T(8,128)(2,1)} %all-gather.20.cloned.1.call-done, bf16[4096,896]{1,0:T(8,128)(2,1)} %all-gather.22.cloned.1.call-done), kind=kOutput, calls=%fused_computation.120 | convolution fusion | flops 3758096384 | bytes 13369344 | tf_op jit(solution)/shard_map/dot_general | solution.py:58
  363.5 37.2 %all-gather.24.cloned.1.call-done = bf16[4096,896]{1,0:T(8,128)(2,1)} async-done(((bf16[512,896]{1,0:T(8,128)(2,1)}), bf16[4096,896]{1,0:T(8,128)(2,1)}) %all-gather.24.cloned.1.call-update) | async-done | bytes 7340048 | tf_op jit(solution)/shard_map/all_gather | solution.py:173
  400.8 47.2 %all-gather.26.cloned.1.call-done = bf16[896,4096]{1,0:T(8,128)(2,1)} async-done(((bf16[896,512]{1,0:T(8,128)(2,1)}), bf16[896,4096]{1,0:T(8,128)(2,1)}) %all-gather.26.cloned.1.call-update) | async-done | bytes 7340048 | tf_op jit(solution)/shard_map/all_gather | solution.py:177
  448.0 16.3 %convolution_convert_fusion = bf16[512,4096]{1,0:T(8,128)(2,1)} fusion(bf16[896,4096]{1,0:T(8,128)(2,1)} %all-gather.26.cloned.1.call-done, f32[512,896]{1,0:T(8,128)S(1)} %fusion.65, bf16[512,4096]{1,0:T(8,128)(2,1)} %all-gather.20.cloned.1.call-done, bf16[4096,896]{1,0:T(8,128)(2,1)} %all-gather.24.cloned.1.call-done), kind=kOutput, calls=%fused_computation.22 | convolution fusion | flops 7521042432 | bytes 24903680 | tf_op jit(solution)/shard_map/dot_general | solution.py:179
  464.3 0.6 copy-done.5
  464.9 0.2 convert_reduce_fusion.1
  465.3 0.1 copy.34
  465.5 0.1 copy.35
  465.7 0.3 reshape.446
  466.0 0.2 convolution_convert_fusion.3
  466.2 0.2 reshape.447
  466.5 0.9 reshape.453
  467.4 3.4 all-to-all-start
  470.7 6.0 %all-to-all-done = bf16[8,2,4096]{2,1,0:T(2,128)(2,1)S(1)} async-done(((bf16[8,2,4096]{2,1,0:T(2,128)(2,1)}), bf16[8,2,4096]{2,1,0:T(2,128)(2,1)S(1)}, u32[]{:S(2)}, u32[]{:S(2)}) %all-to-all-start) | async-done | bytes 131104 | tf_op jit(solution)/shard_map/all_to_all | solution.py:218
  476.8 0.2 reshape.454
  477.0 0.3 reshape.448
  477.3 0.4 convolution_convert_fusion.2
  477.7 1.0 reshape.449
  478.6 63.3 %reduce-scatter.5.cloned.1.call-done = bf16[32,4096]{1,0:T(8,128)(2,1)} async-done(((bf16[512,4096]{1,0:T(8,128)(2,1)}), bf16[32,4096]{1,0:T(8,128)(2,1)}) %reduce-scatter.5.cloned.1.call-update) | async-done | bytes 262160 | tf_op jit(solution)/shard_map/reduce_scatter | solution.py:178
  541.9 1.7 fusion.28
  (56 shorter events, 1.2 us)
Async XLA Ops:
  7.2 57.7 %all-gather.10.cloned.1.call-start = ((), (), s32[]{:S(2)}) async-start(), calls=%async_computation.3 | async-start | bytes 4456448 | tf_op jit(solution)/shard_map/all_gather | solution.py:87
  7.9 66.3 %copy-start.3 = (bf16[512,64]{0,1:T(8,128)(2,1)S(1)}, bf16[512,64]{0,1:T(8,128)(2,1)}, u32[]{:S(2)}) copy-start(bf16[512,64]{0,1:T(8,128)(2,1)} %param.19) | copy-start | bytes 196612
  10.9 93.0 %all-gather.12.cloned.1.call-start = ((), (), s32[]{:S(2)}) async-start(), calls=%async_computation.4 | async-start | bytes 2359296 | tf_op jit(solution)/shard_map/all_gather | solution.py:90
  11.6 106.1 %all-gather.14.cloned.1.call-start = ((), (), s32[]{:S(2)}) async-start(), calls=%async_computation.5 | async-start | bytes 1179648 | tf_op jit(solution)/shard_map/all_gather | solution.py:124
  68.5 4.3 collective-permute-start
  74.1 68.7 %all-gather.16.cloned.1.call-start = ((), (), s32[]{:S(2)}) async-start(), calls=%async_computation.6 | async-start | bytes 1179648 | tf_op jit(solution)/shard_map/all_gather | solution.py:125
  92.0 4.4 collective-permute-start.1
  97.1 72.5 %all-gather.18.cloned.1.call-start = ((), (), s32[]{:S(2)}) async-start(), calls=%async_computation.7 | async-start | bytes 2359296 | tf_op jit(solution)/shard_map/all_gather | solution.py:159
  97.7 154.9 %reduce-scatter.3.cloned.1.call-start = ((), (), s32[]{:S(2)}) async-start(), calls=%async_computation.8 | async-start | bytes 4456448 | tf_op jit(solution)/shard_map/reduce_scatter | solution.py:162
  142.8 5.2 copy-start.6
  174.6 0.8 copy-start.4
  174.6 78.0 %copy-start = (bf16[32,4096]{1,0:T(8,128)(2,1)S(1)}, bf16[32,4096]{1,0:T(8,128)(2,1)}, u32[]{:S(2)}) copy-start(bf16[32,4096]{1,0:T(8,128)(2,1)} %param.14) | copy-start | bytes 786436
  174.6 124.8 %all-gather.22.cloned.1.call-start = ((), (), s32[]{:S(2)}) async-start(), calls=%async_computation.10 | async-start | bytes 8257536 | tf_op jit(solution)/shard_map/all_gather | solution.py:172
  175.3 178.4 %all-gather.20.cloned.1.call-start = ((), (), s32[]{:S(2)}) async-start(), calls=%async_computation.9 | async-start | bytes 4456448 | tf_op jit(solution)/shard_map/all_gather | solution.py:166
  255.5 145.2 %all-gather.24.cloned.1.call-start = ((), (), s32[]{:S(2)}) async-start(), calls=%async_computation.11 | async-start | bytes 8257536 | tf_op jit(solution)/shard_map/all_gather | solution.py:173
  256.3 191.7 %all-gather.26.cloned.1.call-start = ((), (), s32[]{:S(2)}) async-start(), calls=%async_computation.12 | async-start | bytes 8257536 | tf_op jit(solution)/shard_map/all_gather | solution.py:177
  256.9 285.0 %reduce-scatter.5.cloned.1.call-start = ((), (), s32[]{:S(2)}) async-start(), calls=%async_computation.13 | async-start | bytes 4456448 | tf_op jit(solution)/shard_map/reduce_scatter | solution.py:178
  464.2 0.7 copy-start.5
  464.2 1.2 copy-start.2
  464.2 77.7 %copy-start.1 = (bf16[32,4096]{1,0:T(8,128)(2,1)S(1)}, bf16[32,4096]{1,0:T(8,128)(2,1)}, u32[]{:S(2)}) copy-start(bf16[32,4096]{1,0:T(8,128)(2,1)} %reduce-scatter.3.cloned.1.call-done) | copy-start | bytes 786436
  467.4 9.4 %all-to-all-start = ((bf16[8,2,4096]{2,1,0:T(2,128)(2,1)}), bf16[8,2,4096]{2,1,0:T(2,128)(2,1)S(1)}, u32[]{:S(2)}, u32[]{:S(2)}) async-start(bf16[8,2,4096]{2,1,0:T(2,128)(2,1)} %reshape.453), calls=%async_computation.2 | async-start | bytes 262144 | tf_op jit(solution)/shard_map/all_to_all | solution.py:218
Sparse Core Ops, SparseCore 0:
  11.0 53.8 all-gather.9
  66.6 25.7 all-gather.11
  94.1 23.5 all-gather.13
  119.3 23.4 all-gather.15
  144.3 25.2 all-gather.17
  174.7 77.8 reduce-scatter.2
  254.4 44.9 all-gather.21
  302.3 51.3 all-gather.19
  355.5 45.2 all-gather.23
  402.4 45.4 all-gather.25
  464.4 77.4 reduce-scatter.4
where the time goes:
time: 551 us; the launch traced here: 550 us
  waiting for transfers between devices  419 us (76%)
  matrix products  52.7 us (10%)
  blocking collectives  28.8 us (5%)
  other arithmetic  23.6 us (4%)
  between operations  14.8 us (3%)
  starting transfers between devices  7.29 us (1%)
    reduce_scatter x1, waiting for transfers between devices, per_device(): lax.psum_scatter(partial_value.astype(jnp.bfloat16), 'gy', scatter_dimens...  77.2 us
    reduce_scatter x1, waiting for transfers between devices, per_device(): lax.psum_scatter(jnp.dot(hidden, down_full, preferred_element_type=jnp.fl...  63.3 us
    all_gather x1, waiting for transfers between devices, per_device(): lax.all_gather(rms_scale(residual, mlp_gain).astype(jnp.bfloat16), 'gy',...  54.3 us
    all_gather x1, waiting for transfers between devices, per_device(): down_full = lax.all_gather(w_down, 'gx', axis=1, tiled=True)  47.2 us
    all_gather x1, waiting for transfers between devices, per_device(): lax.all_gather(w_gate, 'gx', axis=0, tiled=True)  42.2 us
    all_gather x1, waiting for transfers between devices, per_device(): lax.all_gather(w_up, 'gx', axis=0, tiled=True)  37.2 us
    all_gather x1, waiting for transfers between devices, per_device(): lax.all_gather(rms_scale(tokens, attn_gain).astype(jnp.bfloat16), 'gy', a...  36.9 us
    all_gather x1, waiting for transfers between devices, per_device(): values = lax.all_gather(value_vectors, 'gx', axis=0, tiled=True)  25 us
  transfers between devices with their start and end apart: 14, of which 13 were waited for; matrix products, arithmetic and copies ran while one was open for 10% of the time, Pallas kernels for 0%

commit v1 on v0

--- a/solution.py
+++ b/solution.py
@@ -163,9 +163,25 @@
         partial_value.astype(jnp.bfloat16), "gy", scatter_dimension=0, tiled=True
     ).astype(jnp.float32)
     residual = (tokens.astype(jnp.float32) + share).astype(jnp.bfloat16)
-    mlp_input = lax.all_gather(
-        rms_scale(residual, mlp_gain).astype(jnp.bfloat16), "gy", axis=0, tiled=True
-    )
+    array = rms_scale(residual, mlp_gain).astype(jnp.bfloat16)
+    size, index, span = (lax.axis_size("gy"), lax.axis_index("gy"), array.shape[0])
+    right = [(i, (i + 1) % size) for i in range(size)]
+    left = [(i, (i - 1) % size) for i in range(size)]
+    whole = jnp.zeros((*array.shape[:0], size * span, *array.shape[0 + 1 :]), array.dtype)
+    whole = lax.dynamic_update_slice_in_dim(whole, array, index * span, axis=0)
+    from_left = from_right = array
+    half_2 = size // 2
+    for step in range(1, half_2 + 1):
+        from_left = lax.ppermute(from_left, "gy", right)
+        whole = lax.dynamic_update_slice_in_dim(
+            whole, from_left, (index - step) % size * span, axis=0
+        )
+        if step < size - half_2:
+            from_right = lax.ppermute(from_right, "gy", left)
+            whole = lax.dynamic_update_slice_in_dim(
+                whole, from_right, (index + step) % size * span, axis=0
+            )
+    mlp_input = whole
     gate, up_values = row_products(
         mlp_input,
         (

time: 551 us -> 497 us (0.902)
  waiting for transfers between devices: 419 us -> 314 us
  starting transfers between devices: 7.29 us -> 45.7 us
  local copies, waits for them, and re-layouts: 4.37 us -> 17.8 us
    all_gather x1 -> x0, waiting for transfers between devices: 54.3 us -> none  [per_device(): lax.all_gather(rms_scale(residual, mlp_gain).astype(jnp.bfloat16), 'gy',...]
    all_gather x1, waiting for transfers between devices: 42.2 us -> 0.01 us  [per_device(): lax.all_gather(w_gate, 'gx', axis=0, tiled=True)]
    ppermute x0 -> x15, starting transfers between devices: none -> 38.6 us  [the longest x7 37.4 us: per_device(): from_right = lax.ppermute(from_right, 'gy', left)]
    all_gather x1, waiting for transfers between devices: 37.2 us -> 0.02 us  [per_device(): lax.all_gather(w_up, 'gx', axis=0, tiled=True)]
    ppermute x0 -> x15, waiting for transfers between devices: none -> 35.4 us  [the longest x8 35.3 us: per_device(): from_left = lax.ppermute(from_left, 'gy', right)]
    dynamic_update_slice x0 -> x15, local copies, waits for them, and re-layouts: none -> 10.9 us  [the longest x8 5.87 us: per_device(): lax.dynamic_update_slice_in_dim(whole, from_left, (index - step) % size *...]
  transfers between devices with their start and end apart: 14 -> 28, of which waited for: 13 -> 19; matrix products, arithmetic and copies ran while one was open for 10% -> 13% of each run, Pallas kernels for 0% -> 0%
where the time goes in v1:
time: 497 us
  waiting for transfers between devices  314 us (63%)
  matrix products  52.8 us (11%)
  starting transfers between devices  45.7 us (9%)
  blocking collectives  28.8 us (6%)
  other arithmetic  22.7 us (5%)
  local copies, waits for them, and re-layouts  17.8 us (4%)
  between operations  15.1 us (3%)
    reduce_scatter x1, waiting for transfers between devices, per_device(): lax.psum_scatter(partial_value.astype(jnp.bfloat16), 'gy', scatter_dimens...  75.7 us
    reduce_scatter x1, waiting for transfers between devices, per_device(): lax.psum_scatter(jnp.dot(hidden, down_full, preferred_element_type=jnp.fl...  63.2 us
    all_gather x1, waiting for transfers between devices, per_device(): down_full = lax.all_gather(w_down, 'gx', axis=1, tiled=True)  41.9 us
    ppermute x7, starting transfers between devices, per_device(): from_right = lax.ppermute(from_right, 'gy', left)  37.4 us
    all_gather x1, waiting for transfers between devices, per_device(): lax.all_gather(rms_scale(tokens, attn_gain).astype(jnp.bfloat16), 'gy', a...  36.9 us
    ppermute x8, waiting for transfers between devices, per_device(): from_left = lax.ppermute(from_left, 'gy', right)  35.3 us
    all_gather x1, waiting for transfers between devices, per_device(): values = lax.all_gather(value_vectors, 'gx', axis=0, tiled=True)  25 us
    dot_general x4, matrix products, row_products(): jnp.dot(source, piece, preferred_element_type=jnp.float32)  21.2 us
  transfers between devices with their start and end apart: 28, of which 19 were waited for; matrix products, arithmetic and copies ran while one was open for 13% of the time, Pallas kernels for 0%

profile of v1, /device:TPU:0, one launch (start us, length us, event | category | flops | bytes accessed | tf_op | source)
XLA Modules:
  0.0 496.5 jit_solution(13526527360649365069)
XLA Ops:
  7.9 1.1 fusion.22
  9.1 1.8 fusion.24
  11.7 0.8 reduce-window.9
  13.4 14.6 %all_gather.32 = bf16[4096,64]{0,1:T(8,128)(2,1)S(1)} all-gather(bf16[512,64]{0,1:T(8,128)(2,1)} %param.18), channel_id=1, replica_groups=mesh['gx'=8,'gy'=16] {'gx'}, dimensions={0}, use_global_device_ids=true | all-gather | bytes 589824 | tf_op jit(solution)/shard_map/all_gather | solution.py:95
  28.0 36.9 %all-gather.9.cloned.1.call-done = bf16[512,4096]{1,0:T(8,128)(2,1)} async-done(((bf16[32,4096]{1,0:T(8,128)(2,1)}), bf16[512,4096]{1,0:T(8,128)(2,1)}) %all-gather.9.cloned.1.call-update) | async-done | bytes 4194320 | tf_op jit(solution)/shard_map/all_gather | solution.py:87
  64.9 3.6 fusion.64
  68.5 1.5 collective-permute-start
  70.0 2.8 collective-permute-done
  74.2 14.2 %all_gather.34 = bf16[4096,64]{0,1:T(8,128)(2,1)S(1)} all-gather(bf16[512,64]{0,1:T(8,128)(2,1)S(1)} %copy-done.3), channel_id=1, replica_groups=mesh['gx'=8,'gy'=16] {'gx'}, dimensions={0}, use_global_device_ids=true | all-gather | bytes 589824 | tf_op jit(solution)/shard_map/all_gather | solution.py:96
  88.3 3.6 fusion.68
  92.0 1.8 collective-permute-start.1
  93.8 2.6 collective-permute-done.1
  97.9 3.6 fusion.20
  102.1 1.8 multiply_cosine_fusion
  103.9 4.2 fusion.67
  108.5 1.2 fusion.30
  109.9 7.8 %all-gather.13.cloned.1.call-done = bf16[4096,128]{0,1:T(8,128)(2,1)} async-done(((bf16[512,128]{0,1:T(8,128)(2,1)}), bf16[4096,128]{0,1:T(8,128)(2,1)}) %all-gather.13.cloned.1.call-update) | async-done | bytes 1048592 | tf_op jit(solution)/shard_map/all_gather | solution.py:124
  117.7 25.0 %all-gather.15.cloned.1.call-done = bf16[4096,128]{0,1:T(8,128)(2,1)} async-done(((bf16[512,128]{0,1:T(8,128)(2,1)}), bf16[4096,128]{0,1:T(8,128)(2,1)}) %all-gather.15.cloned.1.call-update) | async-done | bytes 1048592 | tf_op jit(solution)/shard_map/all_gather | solution.py:125
  142.8 14.2 %conditional.1 = (f32[1,2,512]{2,1,0:T(2,128)S(1)}, f32[1,2,512,128]{2,3,1,0:T(8,128)S(1)}) conditional(s32[]{:T(128)} %convert_element_type.114, () %tuple.16, (pred[512,4096]{0,1:T(8,128)(4,1)S(1)}, bf16[512,1,2,128]{3,0,2,1:T(8,128)(2,1)S(1)}, bf16[4096,128]{0,1:T(8,128)(2,1)}, bf16[4096,128]{0,1:T(8,128)(2,1)}) %tuple.17), branch_computations={%region_6.7_spmd, %region_7.10_spmd} | conditional | flops 2202008576 | bytes 63725612 | solution.py:154
  142.8 5.1 %fusion = (f32[2,512]{1,0:T(2,128)S(1)}, f32[4096,512,2]{1,0,2:T(8,128)S(1)}) fusion(pred[512,4096]{0,1:T(8,128)(4,1)S(1)} %get-tuple-element.8, bf16[512,1,2,128]{3,0,2,1:T(8,128)(2,1)S(1)} %get-tuple-element.10, bf16[4096,128]{0,1:T(8,128)(2,1)} %get-tuple-element.28), kind=kOutput, calls=%fused_computation.2 | convolution fusion | flops 1086323712 | bytes 20189184 | tf_op jit(solution)/shard_map/cond/branch_1_fun/qhgd,khd->hgqk/dot_general | solution.py:135
  147.9 4.6 fusion.7
  152.5 4.4 fusion.2
  157.1 12.6 %all-gather.17.cloned.1.call-done = bf16[256,4096]{1,0:T(8,128)(2,1)} async-done(((bf16[256,512]{1,0:T(8,128)(2,1)}), bf16[256,4096]{1,0:T(8,128)(2,1)}) %all-gather.17.cloned.1.call-update) | async-done | bytes 2097168 | tf_op jit(solution)/shard_map/all_gather | solution.py:159
  169.6 4.9 convolution_convert_fusion.1
  176.8 75.7 %reduce-scatter.3.cloned.1.call-done = bf16[32,4096]{1,0:T(8,128)(2,1)} async-done(((bf16[512,4096]{1,0:T(8,128)(2,1)}), bf16[32,4096]{1,0:T(8,128)(2,1)}) %reduce-scatter.3.cloned.1.call-update) | async-done | bytes 262160 | tf_op jit(solution)/shard_map/reduce_scatter | solution.py:162
  252.5 1.2 fusion.26
  253.8 2.5 broadcast_in_dim.22
  256.3 0.8 constant_dynamic-update-slice_fusion.15
  257.2 1.2 collective-permute-start.2
  258.3 4.2 collective-permute-start.3
  262.5 4.4 collective-permute-done.2
  266.9 5.3 %collective-permute-start.5 = (bf16[32,4096]{1,0:T(8,128)(2,1)S(1)}, bf16[32,4096]{1,0:T(8,128)(2,1)S(1)}, u32[]{:S(2)}, u32[]{:S(2)}) collective-permute-start(bf16[32,4096]{1,0:T(8,128)(2,1)S(1)} %collective-permute-done.3), channel_id=1, source_target_pairs={{0,15},{1,0},{2,1},{3,2},{4,3},{5,4},{6,5},{7,6},{8,7},{9,8},{10,9... | collective-permute-start | bytes 786440 | tf_op jit(solution)/shard_map/ppermute | solution.py:180
  272.2 0.7 constant_dynamic-update-slice_fusion.14
  273.0 0.7 constant_dynamic-update-slice_fusion.13
  273.7 2.9 collective-permute-done.4
  276.6 5.3 %collective-permute-start.7 = (bf16[32,4096]{1,0:T(8,128)(2,1)S(1)}, bf16[32,4096]{1,0:T(8,128)(2,1)S(1)}, u32[]{:S(2)}, u32[]{:S(2)}) collective-permute-start(bf16[32,4096]{1,0:T(8,128)(2,1)S(1)} %collective-permute-done.5), channel_id=1, source_target_pairs={{0,15},{1,0},{2,1},{3,2},{4,3},{5,4},{6,5},{7,6},{8,7},{9,8},{10,9... | collective-permute-start | bytes 786440 | tf_op jit(solution)/shard_map/ppermute | solution.py:180
  281.9 0.7 constant_dynamic-update-slice_fusion.12
  282.7 0.7 constant_dynamic-update-slice_fusion.11
  283.4 2.9 collective-permute-done.6
  286.3 5.3 %collective-permute-start.9 = (bf16[32,4096]{1,0:T(8,128)(2,1)S(1)}, bf16[32,4096]{1,0:T(8,128)(2,1)S(1)}, u32[]{:S(2)}, u32[]{:S(2)}) collective-permute-start(bf16[32,4096]{1,0:T(8,128)(2,1)S(1)} %collective-permute-done.7), channel_id=1, source_target_pairs={{0,15},{1,0},{2,1},{3,2},{4,3},{5,4},{6,5},{7,6},{8,7},{9,8},{10,9... | collective-permute-start | bytes 786440 | tf_op jit(solution)/shard_map/ppermute | solution.py:180
  291.6 0.7 constant_dynamic-update-slice_fusion.10
  293.1 3.3 collective-permute-done.8
  296.4 5.6 %collective-permute-start.11 = (bf16[32,4096]{1,0:T(8,128)(2,1)S(1)}, bf16[32,4096]{1,0:T(8,128)(2,1)S(1)}, u32[]{:S(2)}, u32[]{:S(2)}) collective-permute-start(bf16[32,4096]{1,0:T(8,128)(2,1)S(1)} %collective-permute-done.9), channel_id=1, source_target_pairs={{0,15},{1,0},{2,1},{3,2},{4,3},{5,4},{6,5},{7,6},{8,7},{9,8},{10,9... | collective-permute-start | bytes 786440 | tf_op jit(solution)/shard_map/ppermute | solution.py:180
  302.1 0.7 constant_dynamic-update-slice_fusion.8
  302.8 0.7 constant_dynamic-update-slice_fusion.7
  303.5 4.2 collective-permute-done.10
  307.8 5.8 %collective-permute-start.13 = (bf16[32,4096]{1,0:T(8,128)(2,1)S(1)}, bf16[32,4096]{1,0:T(8,128)(2,1)S(1)}, u32[]{:S(2)}, u32[]{:S(2)}) collective-permute-start(bf16[32,4096]{1,0:T(8,128)(2,1)S(1)} %collective-permute-done.11), channel_id=1, source_target_pairs={{0,15},{1,0},{2,1},{3,2},{4,3},{5,4},{6,5},{7,6},{8,7},{9,8},{10,9... | collective-permute-start | bytes 786440 | tf_op jit(solution)/shard_map/ppermute | solution.py:180
  314.4 0.7 constant_dynamic-update-slice_fusion.5
  315.1 5.0 %collective-permute-done.12 = bf16[32,4096]{1,0:T(8,128)(2,1)S(1)} collective-permute-done((bf16[32,4096]{1,0:T(8,128)(2,1)S(1)}, bf16[32,4096]{1,0:T(8,128)(2,1)S(1)}, u32[]{:S(2)}, u32[]{:S(2)}) %collective-permute-start.12) | collective-permute-done | bytes 262176 | tf_op jit(solution)/shard_map/ppermute | solution.py:175
  320.1 5.8 %collective-permute-start.15 = (bf16[32,4096]{1,0:T(8,128)(2,1)S(1)}, bf16[32,4096]{1,0:T(8,128)(2,1)S(1)}, u32[]{:S(2)}, u32[]{:S(2)}) collective-permute-start(bf16[32,4096]{1,0:T(8,128)(2,1)S(1)} %collective-permute-done.13), channel_id=1, source_target_pairs={{0,15},{1,0},{2,1},{3,2},{4,3},{5,4},{6,5},{7,6},{8,7},{9,8},{10,9... | collective-permute-start | bytes 786440 | tf_op jit(solution)/shard_map/ppermute | solution.py:180
  325.9 0.7 constant_dynamic-update-slice_fusion.4
  327.4 4.4 collective-permute-done.14
  331.8 0.7 constant_dynamic-update-slice_fusion.2
  333.2 8.2 %collective-permute-done.16 = bf16[32,4096]{1,0:T(8,128)(2,1)S(1)} collective-permute-done((bf16[32,4096]{1,0:T(8,128)(2,1)S(1)}, bf16[32,4096]{1,0:T(8,128)(2,1)S(1)}, u32[]{:S(2)}, u32[]{:S(2)}) %collective-permute-start.16) | collective-permute-done | bytes 262176 | tf_op jit(solution)/shard_map/ppermute | solution.py:175
  341.4 0.7 constant_dynamic-update-slice_fusion
  342.2 9.9 %fusion.69 = f32[512,896]{1,0:T(8,128)S(1)} fusion(bf16[512,4096]{1,0:T(8,128)(2,1)} %constant_dynamic-update-slice_fusion, bf16[4096,896]{1,0:T(8,128)(2,1)} %all-gather.19.cloned.1.call-done), kind=kOutput, calls=%fused_computation.138 | convolution fusion | flops 3758096384 | bytes 13369344 | tf_op jit(solution)/shard_map/dot_general | solution.py:58
  352.1 41.9 %all-gather.23.cloned.1.call-done = bf16[896,4096]{1,0:T(8,128)(2,1)} async-done(((bf16[896,512]{1,0:T(8,128)(2,1)}), bf16[896,4096]{1,0:T(8,128)(2,1)}) %all-gather.23.cloned.1.call-update) | async-done | bytes 7340048 | tf_op jit(solution)/shard_map/all_gather | solution.py:193
  394.0 16.3 %convolution_convert_fusion = bf16[512,4096]{1,0:T(8,128)(2,1)} fusion(bf16[896,4096]{1,0:T(8,128)(2,1)} %all-gather.23.cloned.1.call-done, f32[512,896]{1,0:T(8,128)S(1)} %fusion.69, bf16[512,4096]{1,0:T(8,128)(2,1)} %constant_dynamic-update-slice_fusion, bf16[4096,896]{1,0:T(8,128)(2,1)} %all-gather.21.cloned.1.call-done), kind=kOutput, calls=%fused_computation.22 | convolution fusion | flops 7521042432 | bytes 24903680 | tf_op jit(solution)/shard_map/dot_general | solution.py:195
  412.5 0.9 reshape.453
  413.4 3.4 all-to-all-start
  416.8 6.0 %all-to-all-done = bf16[8,2,4096]{2,1,0:T(2,128)(2,1)S(1)} async-done(((bf16[8,2,4096]{2,1,0:T(2,128)(2,1)}), bf16[8,2,4096]{2,1,0:T(2,128)(2,1)S(1)}, u32[]{:S(2)}, u32[]{:S(2)}) %all-to-all-start) | async-done | bytes 131104 | tf_op jit(solution)/shard_map/all_to_all | solution.py:234
  423.7 1.0 reshape.449
  424.7 63.2 %reduce-scatter.5.cloned.1.call-done = bf16[32,4096]{1,0:T(8,128)(2,1)} async-done(((bf16[512,4096]{1,0:T(8,128)(2,1)}), bf16[32,4096]{1,0:T(8,128)(2,1)}) %reduce-scatter.5.cloned.1.call-update) | async-done | bytes 262160 | tf_op jit(solution)/shard_map/reduce_scatter | solution.py:194
  487.9 1.7 fusion.29
  (99 shorter events, 14.1 us)
Async XLA Ops:
  7.2 57.7 %all-gather.9.cloned.1.call-start = ((), (), s32[]{:S(2)}) async-start(), calls=%async_computation.3 | async-start | bytes 4456448 | tf_op jit(solution)/shard_map/all_gather | solution.py:87
  7.9 66.3 %copy-start.3 = (bf16[512,64]{0,1:T(8,128)(2,1)S(1)}, bf16[512,64]{0,1:T(8,128)(2,1)}, u32[]{:S(2)}) copy-start(bf16[512,64]{0,1:T(8,128)(2,1)} %param.19) | copy-start | bytes 196612
  10.9 93.0 %all-gather.11.cloned.1.call-start = ((), (), s32[]{:S(2)}) async-start(), calls=%async_computation.4 | async-start | bytes 2359296 | tf_op jit(solution)/shard_map/all_gather | solution.py:90
  11.6 106.1 %all-gather.13.cloned.1.call-start = ((), (), s32[]{:S(2)}) async-start(), calls=%async_computation.5 | async-start | bytes 1179648 | tf_op jit(solution)/shard_map/all_gather | solution.py:124
  68.5 4.3 collective-permute-start
  74.1 68.7 %all-gather.15.cloned.1.call-start = ((), (), s32[]{:S(2)}) async-start(), calls=%async_computation.6 | async-start | bytes 1179648 | tf_op jit(solution)/shard_map/all_gather | solution.py:125
  92.0 4.4 collective-permute-start.1
  97.1 72.5 %all-gather.17.cloned.1.call-start = ((), (), s32[]{:S(2)}) async-start(), calls=%async_computation.7 | async-start | bytes 2359296 | tf_op jit(solution)/shard_map/all_gather | solution.py:159
  97.7 154.8 %reduce-scatter.3.cloned.1.call-start = ((), (), s32[]{:S(2)}) async-start(), calls=%async_computation.8 | async-start | bytes 4456448 | tf_op jit(solution)/shard_map/reduce_scatter | solution.py:162
  142.8 5.2 %copy-start.6 = (bf16[4096,128]{0,1:T(8,128)(2,1)S(1)}, bf16[4096,128]{0,1:T(8,128)(2,1)}, u32[]{:S(2)}) copy-start(bf16[4096,128]{0,1:T(8,128)(2,1)} %get-tuple-element.29) | copy-start | bytes 3145732 | tf_op jit(solution)/shard_map/cond
  174.5 2.3 copy-start.4
  174.5 78.0 %copy-start = (bf16[32,4096]{1,0:T(8,128)(2,1)S(1)}, bf16[32,4096]{1,0:T(8,128)(2,1)}, u32[]{:S(2)}) copy-start(bf16[32,4096]{1,0:T(8,128)(2,1)} %param.14) | copy-start | bytes 786436
  174.5 167.6 %all-gather.19.cloned.1.call-start = ((), (), s32[]{:S(2)}) async-start(), calls=%async_computation.9 | async-start | bytes 8257536 | tf_op jit(solution)/shard_map/all_gather | solution.py:188
  175.3 176.8 %all-gather.21.cloned.1.call-start = ((), (), s32[]{:S(2)}) async-start(), calls=%async_computation.10 | async-start | bytes 8257536 | tf_op jit(solution)/shard_map/all_gather | solution.py:189
  176.0 217.9 %all-gather.23.cloned.1.call-start = ((), (), s32[]{:S(2)}) async-start(), calls=%async_computation.11 | async-start | bytes 8257536 | tf_op jit(solution)/shard_map/all_gather | solution.py:193
  176.8 311.1 %reduce-scatter.5.cloned.1.call-start = ((), (), s32[]{:S(2)}) async-start(), calls=%async_computation.12 | async-start | bytes 4456448 | tf_op jit(solution)/shard_map/reduce_scatter | solution.py:194
  252.5 3.8 copy-start.1
  257.2 9.7 %collective-permute-start.2 = (bf16[32,4096]{1,0:T(8,128)(2,1)S(1)}, bf16[32,4096]{1,0:T(8,128)(2,1)S(1)}, u32[]{:S(2)}, u32[]{:S(2)}) collective-permute-start(bf16[32,4096]{1,0:T(8,128)(2,1)S(1)} %get-tuple-element.32), channel_id=1, source_target_pairs={{0,1},{1,2},{2,3},{3,4},{4,5},{5,6},{6,7},{7,8},{8,9},{9,10},{10,1... | collective-permute-start | bytes 786440 | tf_op jit(solution)/shard_map/ppermute | solution.py:175
  258.3 8.6 %collective-permute-start.3 = (bf16[32,4096]{1,0:T(8,128)(2,1)S(1)}, bf16[32,4096]{1,0:T(8,128)(2,1)S(1)}, u32[]{:S(2)}, u32[]{:S(2)}) collective-permute-start(bf16[32,4096]{1,0:T(8,128)(2,1)S(1)} %get-tuple-element.32), channel_id=1, source_target_pairs={{0,15},{1,0},{2,1},{3,2},{4,3},{5,4},{6,5},{7,6},{8,7},{9,8},{10,9... | collective-permute-start | bytes 786440 | tf_op jit(solution)/shard_map/ppermute | solution.py:180
  266.9 9.7 %collective-permute-start.4 = (bf16[32,4096]{1,0:T(8,128)(2,1)S(1)}, bf16[32,4096]{1,0:T(8,128)(2,1)S(1)}, u32[]{:S(2)}, u32[]{:S(2)}) collective-permute-start(bf16[32,4096]{1,0:T(8,128)(2,1)S(1)} %collective-permute-done.2), channel_id=1, source_target_pairs={{0,1},{1,2},{2,3},{3,4},{4,5},{5,6},{6,7},{7,8},{8,9},{9,10},{10,1... | collective-permute-start | bytes 786440 | tf_op jit(solution)/shard_map/ppermute | solution.py:175
  266.9 9.7 %collective-permute-start.5 = (bf16[32,4096]{1,0:T(8,128)(2,1)S(1)}, bf16[32,4096]{1,0:T(8,128)(2,1)S(1)}, u32[]{:S(2)}, u32[]{:S(2)}) collective-permute-start(bf16[32,4096]{1,0:T(8,128)(2,1)S(1)} %collective-permute-done.3), channel_id=1, source_target_pairs={{0,15},{1,0},{2,1},{3,2},{4,3},{5,4},{6,5},{7,6},{8,7},{9,8},{10,9... | collective-permute-start | bytes 786440 | tf_op jit(solution)/shard_map/ppermute | solution.py:180
  276.6 9.7 %collective-permute-start.6 = (bf16[32,4096]{1,0:T(8,128)(2,1)S(1)}, bf16[32,4096]{1,0:T(8,128)(2,1)S(1)}, u32[]{:S(2)}, u32[]{:S(2)}) collective-permute-start(bf16[32,4096]{1,0:T(8,128)(2,1)S(1)} %collective-permute-done.4), channel_id=1, source_target_pairs={{0,1},{1,2},{2,3},{3,4},{4,5},{5,6},{6,7},{7,8},{8,9},{9,10},{10,1... | collective-permute-start | bytes 786440 | tf_op jit(solution)/shard_map/ppermute | solution.py:175
  276.6 9.7 %collective-permute-start.7 = (bf16[32,4096]{1,0:T(8,128)(2,1)S(1)}, bf16[32,4096]{1,0:T(8,128)(2,1)S(1)}, u32[]{:S(2)}, u32[]{:S(2)}) collective-permute-start(bf16[32,4096]{1,0:T(8,128)(2,1)S(1)} %collective-permute-done.5), channel_id=1, source_target_pairs={{0,15},{1,0},{2,1},{3,2},{4,3},{5,4},{6,5},{7,6},{8,7},{9,8},{10,9... | collective-permute-start | bytes 786440 | tf_op jit(solution)/shard_map/ppermute | solution.py:180
  286.3 10.1 %collective-permute-start.8 = (bf16[32,4096]{1,0:T(8,128)(2,1)S(1)}, bf16[32,4096]{1,0:T(8,128)(2,1)S(1)}, u32[]{:S(2)}, u32[]{:S(2)}) collective-permute-start(bf16[32,4096]{1,0:T(8,128)(2,1)S(1)} %collective-permute-done.6), channel_id=1, source_target_pairs={{0,1},{1,2},{2,3},{3,4},{4,5},{5,6},{6,7},{7,8},{8,9},{9,10},{10,1... | collective-permute-start | bytes 786440 | tf_op jit(solution)/shard_map/ppermute | solution.py:175
  286.3 10.1 %collective-permute-start.9 = (bf16[32,4096]{1,0:T(8,128)(2,1)S(1)}, bf16[32,4096]{1,0:T(8,128)(2,1)S(1)}, u32[]{:S(2)}, u32[]{:S(2)}) collective-permute-start(bf16[32,4096]{1,0:T(8,128)(2,1)S(1)} %collective-permute-done.7), channel_id=1, source_target_pairs={{0,15},{1,0},{2,1},{3,2},{4,3},{5,4},{6,5},{7,6},{8,7},{9,8},{10,9... | collective-permute-start | bytes 786440 | tf_op jit(solution)/shard_map/ppermute | solution.py:180
  296.4 11.3 %collective-permute-start.10 = (bf16[32,4096]{1,0:T(8,128)(2,1)S(1)}, bf16[32,4096]{1,0:T(8,128)(2,1)S(1)}, u32[]{:S(2)}, u32[]{:S(2)}) collective-permute-start(bf16[32,4096]{1,0:T(8,128)(2,1)S(1)} %collective-permute-done.8), channel_id=1, source_target_pairs={{0,1},{1,2},{2,3},{3,4},{4,5},{5,6},{6,7},{7,8},{8,9},{9,10},{10,1... | collective-permute-start | bytes 786440 | tf_op jit(solution)/shard_map/ppermute | solution.py:175
  296.4 11.4 %collective-permute-start.11 = (bf16[32,4096]{1,0:T(8,128)(2,1)S(1)}, bf16[32,4096]{1,0:T(8,128)(2,1)S(1)}, u32[]{:S(2)}, u32[]{:S(2)}) collective-permute-start(bf16[32,4096]{1,0:T(8,128)(2,1)S(1)} %collective-permute-done.9), channel_id=1, source_target_pairs={{0,15},{1,0},{2,1},{3,2},{4,3},{5,4},{6,5},{7,6},{8,7},{9,8},{10,9... | collective-permute-start | bytes 786440 | tf_op jit(solution)/shard_map/ppermute | solution.py:180
  307.7 12.4 %collective-permute-start.12 = (bf16[32,4096]{1,0:T(8,128)(2,1)S(1)}, bf16[32,4096]{1,0:T(8,128)(2,1)S(1)}, u32[]{:S(2)}, u32[]{:S(2)}) collective-permute-start(bf16[32,4096]{1,0:T(8,128)(2,1)S(1)} %collective-permute-done.10), channel_id=1, source_target_pairs={{0,1},{1,2},{2,3},{3,4},{4,5},{5,6},{6,7},{7,8},{8,9},{9,10},{10,1... | collective-permute-start | bytes 786440 | tf_op jit(solution)/shard_map/ppermute | solution.py:175
  307.8 12.3 %collective-permute-start.13 = (bf16[32,4096]{1,0:T(8,128)(2,1)S(1)}, bf16[32,4096]{1,0:T(8,128)(2,1)S(1)}, u32[]{:S(2)}, u32[]{:S(2)}) collective-permute-start(bf16[32,4096]{1,0:T(8,128)(2,1)S(1)} %collective-permute-done.11), channel_id=1, source_target_pairs={{0,15},{1,0},{2,1},{3,2},{4,3},{5,4},{6,5},{7,6},{8,7},{9,8},{10,9... | collective-permute-start | bytes 786440 | tf_op jit(solution)/shard_map/ppermute | solution.py:180
  320.1 11.6 %collective-permute-start.14 = (bf16[32,4096]{1,0:T(8,128)(2,1)S(1)}, bf16[32,4096]{1,0:T(8,128)(2,1)S(1)}, u32[]{:S(2)}, u32[]{:S(2)}) collective-permute-start(bf16[32,4096]{1,0:T(8,128)(2,1)S(1)} %collective-permute-done.12), channel_id=1, source_target_pairs={{0,1},{1,2},{2,3},{3,4},{4,5},{5,6},{6,7},{7,8},{8,9},{9,10},{10,1... | collective-permute-start | bytes 786440 | tf_op jit(solution)/shard_map/ppermute | solution.py:175
  320.1 12.4 %collective-permute-start.15 = (bf16[32,4096]{1,0:T(8,128)(2,1)S(1)}, bf16[32,4096]{1,0:T(8,128)(2,1)S(1)}, u32[]{:S(2)}, u32[]{:S(2)}) collective-permute-start(bf16[32,4096]{1,0:T(8,128)(2,1)S(1)} %collective-permute-done.13), channel_id=1, source_target_pairs={{0,15},{1,0},{2,1},{3,2},{4,3},{5,4},{6,5},{7,6},{8,7},{9,8},{10,9... | collective-permute-start | bytes 786440 | tf_op jit(solution)/shard_map/ppermute | solution.py:180
  331.8 9.7 %collective-permute-start.16 = (bf16[32,4096]{1,0:T(8,128)(2,1)S(1)}, bf16[32,4096]{1,0:T(8,128)(2,1)S(1)}, u32[]{:S(2)}, u32[]{:S(2)}) collective-permute-start(bf16[32,4096]{1,0:T(8,128)(2,1)S(1)} %collective-permute-done.14), channel_id=1, source_target_pairs={{0,1},{1,2},{2,3},{3,4},{4,5},{5,6},{6,7},{7,8},{8,9},{9,10},{10,1... | collective-permute-start | bytes 786440 | tf_op jit(solution)/shard_map/ppermute | solution.py:175
  410.3 0.7 copy-start.5
  410.3 1.2 copy-start.2
  413.4 9.4 %all-to-all-start = ((bf16[8,2,4096]{2,1,0:T(2,128)(2,1)}), bf16[8,2,4096]{2,1,0:T(2,128)(2,1)S(1)}, u32[]{:S(2)}, u32[]{:S(2)}) async-start(bf16[8,2,4096]{2,1,0:T(2,128)(2,1)} %reshape.453), calls=%async_computation.2 | async-start | bytes 262144 | tf_op jit(solution)/shard_map/all_to_all | solution.py:234
Sparse Core Ops, SparseCore 0:
  11.0 53.8 all-gather.8
  66.6 25.7 all-gather.10
  94.1 23.5 all-gather.12
  119.3 23.4 all-gather.14
  144.3 25.2 all-gather.16
  174.7 77.8 reduce-scatter.2
  254.3 44.9 all-gather.18
  301.1 45.4 all-gather.20
  348.4 45.4 all-gather.22
  410.4 77.4 reduce-scatter.4
